TPU v7x, 32 devices: a whole 2x2x4 slice. The times are simulated.
32 devices in a mesh: row: 8 (over z, y), col: 4 (over x, core).
Axes of the slice: x: 2, y: 2, z: 4, core: 2. Of those that a mesh axis runs over, the one named last changes fastest.
Arguments:
- momentum: float32 [8192, 8192], P('row', 'col'), may hold values from -6 to 6
- gradient: bfloat16 [8192, 8192], P('row', 'col'), may hold values from -6 to 6
- weight: bfloat16 [8192, 8192], P('row', 'col'), may hold values from -6 to 6
- right_start: float32 [8192, 512], P('col', 'row'), may hold values from -0.0625 to 0.0625
Outputs:
- new_momentum: float32 [8192, 8192], P('row', 'col')
- new_weight: bfloat16 [8192, 8192], P('row', 'col')
- new_right: float32 [8192, 512], P('col', 'row')
All inputs are finite; a program needn't handle non-finite values.
Results may differ from a plain program's by a relative error of at most 0.001.
Values sent between devices are 32-bit elements; how exact they have to be, the bound alone decides.
A program may use at most 128 MiB of HBM per device.

v0:
```python
import jax
import jax.numpy as jnp
from jax import lax
from jax.sharding import PartitionSpec as P

ITERS = 2
BLOCK = 128
gram_mode = lax.Precision.HIGHEST
wide_mode = lax.Precision.HIGH
momentum_decay = 0.9
step_rate = 0.1
epsilon = 1e-06


def self_gram(rows):
    return lax.dot_general(rows, rows, (((0,), (0,)), ((), ())), precision=gram_mode)


def times_transposed(a, b):
    return lax.dot_general(a, b, (((1,), (1,)), ((), ())), precision=gram_mode)


def solve_rows(rows, gram_sum):
    rank = gram_sum.shape[0]
    block = min(BLOCK, rank)
    trailing = gram_sum
    rest = rows
    solved = []
    for at in range(0, rank, block):
        size = min(block, rank - at)
        corner = lax.linalg.cholesky(trailing[:size, :size], symmetrize_input=False)
        inverse = lax.linalg.triangular_solve(
            corner, jnp.eye(size, dtype=corner.dtype), left_side=True, lower=True
        )
        block_rows = times_transposed(rest[:, :size], inverse)
        solved.append(block_rows)
        if at + size < rank:
            panel = times_transposed(trailing[size:, :size], inverse)
            trailing = trailing[size:, size:] - times_transposed(panel, panel)
            rest = rest[:, size:] - times_transposed(block_rows, panel)
    return jnp.concatenate(solved, axis=1)


def shards(momentum, gradient, weight, right_start):
    rows_at, cols_at = (lax.psum(1, "row"), lax.psum(1, "col"))
    out_dim, in_dim = (momentum.shape[0] * rows_at, momentum.shape[1] * cols_at)
    rank = right_start.shape[1] * rows_at
    blended = momentum + gradient.astype(jnp.float32)
    right_full = lax.all_gather(right_start, "row", axis=1, tiled=True)
    right_shard = right_start
    for iteration in range(ITERS):
        partials = jnp.dot(blended, right_full, precision=wide_mode)
        left_sum = lax.psum(partials, "col")
        gram_sum = lax.psum(self_gram(left_sum), "row")
        left_rows = solve_rows(left_sum, gram_sum)
        transposed = lax.dot_general(
            blended, left_rows, (((0,), (0,)), ((), ())), precision=wide_mode
        )
        products = lax.psum_scatter(transposed, "row", scatter_dimension=1, tiled=True)
        squares = lax.psum(jnp.sum(products * products, axis=0, keepdims=True), "col")
        col_norms = jnp.sqrt(squares + epsilon)
        right_shard = products / col_norms
        products_full, norms_full = (
            lax.all_gather(products, "row", axis=1, tiled=True),
            lax.all_gather(col_norms, "row", axis=1, tiled=True),
        )
        right_full = products_full / norms_full
    outer_dims = (((1,), (1,)), ((), ()))
    feedback = lax.dot_general(left_rows, products_full, outer_dims, precision=wide_mode)
    new_momentum = blended - (1.0 - momentum_decay) * feedback
    scale_factor = step_rate * (out_dim * in_dim / rank) ** 0.5
    update = lax.dot_general(left_rows, right_full, outer_dims, precision=wide_mode)
    new_weight = (weight.astype(jnp.float32) - scale_factor * update).astype(jnp.bfloat16)
    return (new_momentum, new_weight, right_shard)


def solution(mesh):
    return jax.shard_map(
        shards,
        mesh=mesh,
        in_specs=(P("row", "col"), P("row", "col"), P("row", "col"), P("col", "row")),
        out_specs=(P("row", "col"), P("row", "col"), P("col", "row")),
        check_vma=False,
    )
```

profile of v0, /device:TPU:0, one launch (start us, length us, event | category | flops | bytes accessed | tf_op | source)
XLA Modules:
  0.0 969.1 jit_solution(15669869728964990464)
XLA Ops:
  7.9 77.7 %all-gather.4.cloned.1.call-done = f32[2048,512]{0,1:T(8,128)} async-done(((f32[2048,64]{0,1:T(8,128)}), f32[2048,512]{0,1:T(8,128)}) %all-gather.4.cloned.1.call-update) | async-done | bytes 4194320 | tf_op jit(solution)/shard_map/all_gather | solution.py:49
  85.7 12.0 %fusion.75 = f32[1024,512]{1,0:T(8,128)} fusion(f32[2048,512]{0,1:T(8,128)} %all-gather.4.cloned.1.call-done, f32[1024,2048]{1,0:T(8,128)} %param.7, bf16[1024,2048]{1,0:T(8,128)(2,1)} %param.8), kind=kOutput, calls=%fused_computation.122 | convolution fusion | flops 6446645248 | bytes 18874368 | tf_op jit(solution)/shard_map/dot_general | solution.py:52
  97.7 50.0 %all-reduce.7.cloned.1.call-done = f32[1024,512]{1,0:T(8,128)} async-done(((f32[1024,512]{1,0:T(8,128)}), f32[1024,512]{1,0:T(8,128)}) %all-reduce.7.cloned.1.call-update) | async-done | bytes 2097168 | tf_op jit(solution)/shard_map/psum | solution.py:53
  154.7 78.3 %all-reduce.9.cloned.1.call-done = f32[512,512]{1,0:T(8,128)} async-done(((f32[512,512]{1,0:T(8,128)}), f32[512,512]{1,0:T(8,128)}) %all-reduce.9.cloned.1.call-update) | async-done | bytes 1048592 | tf_op jit(solution)/shard_map/psum | solution.py:54
  233.8 11.7 %custom-call.20 = f32[128,128]{1,0:T(8,128)S(1)} custom-call(f32[128,128]{1,0:T(8,128)S(1)} %slice.125), custom_call_target="Cholesky" | custom-call | tf_op jit(solution)/shard_map/cholesky/custom-call.1 | solution.py:31
  246.9 9.8 %custom-call.21 = f32[1,128,128]{1,2,0:T(8,128)S(1)} custom-call(f32[1,128,128]{2,1,0:T(8,128)S(1)} %fusion.50), custom_call_target="InvertDiagBlocksLowerTriangular" | custom-call | tf_op jit(solution)/shard_map/triangular_solve/custom-call.0 | solution.py:32
  259.9 11.7 %custom-call.22 = f32[128,128]{1,0:T(8,128)S(1)} custom-call(f32[128,128]{1,0:T(8,128)S(1)} %slice.130), custom_call_target="Cholesky" | custom-call | tf_op jit(solution)/shard_map/cholesky/custom-call.1 | solution.py:31
  273.0 10.2 %custom-call.23 = f32[1,128,128]{1,2,0:T(8,128)S(1)} custom-call(f32[1,128,128]{2,1,0:T(8,128)S(1)} %fusion.51), custom_call_target="InvertDiagBlocksLowerTriangular" | custom-call | tf_op jit(solution)/shard_map/triangular_solve/custom-call.0 | solution.py:32
  284.2 11.7 %custom-call.24 = f32[128,128]{1,0:T(8,128)S(1)} custom-call(f32[128,128]{1,0:T(8,128)S(1)} %slice.135), custom_call_target="Cholesky" | custom-call | tf_op jit(solution)/shard_map/cholesky/custom-call.1 | solution.py:31
  297.2 9.8 %custom-call.25 = f32[1,128,128]{1,2,0:T(8,128)S(1)} custom-call(f32[1,128,128]{2,1,0:T(8,128)S(1)} %fusion.52), custom_call_target="InvertDiagBlocksLowerTriangular" | custom-call | tf_op jit(solution)/shard_map/triangular_solve/custom-call.0 | solution.py:32
  307.9 11.7 %custom-call.26 = f32[128,128]{1,0:T(8,128)S(1)} custom-call(f32[128,128]{1,0:T(8,128)S(1)} %convolution_subtract_fusion.9), custom_call_target="Cholesky" | custom-call | tf_op jit(solution)/shard_map/cholesky/custom-call.1 | solution.py:31
  320.9 10.0 %custom-call.27 = f32[1,128,128]{1,2,0:T(8,128)S(1)} custom-call(f32[1,128,128]{2,1,0:T(8,128)S(1)} %fusion.53), custom_call_target="InvertDiagBlocksLowerTriangular" | custom-call | tf_op jit(solution)/shard_map/triangular_solve/custom-call.0 | solution.py:32
  337.7 11.1 %fusion.3 = f32[2048,512]{0,1:T(8,128)} fusion(f32[1024,128]{0,1:T(8,128)S(1)} %fusion.77, f32[1024,128]{0,1:T(8,128)S(1)} %fusion.19, f32[1024,128]{0,1:T(8,128)S(1)} %fusion.21, f32[1024,128]{0,1:T(8,128)S(1)} %fusion.23, f32[1024,2048]{1,0:T(8,128)} %param.7, bf16[1024,2048]{1,0:T(8,128)(2,1)S(1)} %copy-done), kind=kOutput, calls=%fused_computation.6 | convolution fusion | flops 6448218112 | bytes 18874368 | tf_op jit(solution)/shard_map/dot_general | solution.py:56
  348.8 88.0 %reduce-scatter.3.cloned.1.call-done = f32[2048,64]{0,1:T(8,128)} async-done(((f32[2048,512]{0,1:T(8,128)}), f32[2048,64]{0,1:T(8,128)}) %reduce-scatter.3.cloned.1.call-update) | async-done | bytes 524304 | tf_op jit(solution)/shard_map/reduce_scatter | solution.py:59
  445.6 21.6 %all-reduce = f32[512]{0:T(512)S(1)} all-reduce(f32[512]{0:T(512)S(1)} %bitcast_dynamic-update-slice_fusion), channel_id=1, replica_groups=mesh['row'=8,'col'=4] {'row'}, use_global_device_ids=true, to_apply=%add | all-reduce | flops 512 | bytes 4096
  467.2 44.4 %all-gather.6.cloned.1.call-done = f32[2048,512]{0,1:T(8,128)} async-done(((f32[2048,64]{0,1:T(8,128)}), f32[2048,512]{0,1:T(8,128)}) %all-gather.6.cloned.1.call-update) | async-done | bytes 4194320 | tf_op jit(solution)/shard_map/all_gather | solution.py:64
  511.6 12.2 %fusion.1 = f32[1024,512]{1,0:T(8,128)} fusion(f32[2048,512]{0,1:T(8,128)} %all-gather.6.cloned.1.call-done, f32[512]{0:T(512)S(1)} %all-reduce, f32[1024,2048]{1,0:T(8,128)} %param.7, bf16[1024,2048]{1,0:T(8,128)(2,1)} %param.8), kind=kOutput, calls=%fused_computation.4 | convolution fusion | flops 6447693824 | bytes 18876416 | tf_op jit(solution)/shard_map/dot_general | solution.py:52
  523.8 50.0 %all-reduce.11.cloned.1.call-done = f32[1024,512]{1,0:T(8,128)} async-done(((f32[1024,512]{1,0:T(8,128)}), f32[1024,512]{1,0:T(8,128)}) %all-reduce.11.cloned.1.call-update) | async-done | bytes 2097168 | tf_op jit(solution)/shard_map/psum | solution.py:53
  581.0 78.1 %all-reduce.13.cloned.1.call-done = f32[512,512]{1,0:T(8,128)} async-done(((f32[512,512]{1,0:T(8,128)}), f32[512,512]{1,0:T(8,128)}) %all-reduce.13.cloned.1.call-update) | async-done | bytes 1048592 | tf_op jit(solution)/shard_map/psum | solution.py:54
  659.9 11.7 %custom-call.28 = f32[128,128]{1,0:T(8,128)S(1)} custom-call(f32[128,128]{1,0:T(8,128)S(1)} %slice.140), custom_call_target="Cholesky" | custom-call | tf_op jit(solution)/shard_map/cholesky/custom-call.1 | solution.py:31
  672.9 9.8 %custom-call.29 = f32[1,128,128]{1,2,0:T(8,128)S(1)} custom-call(f32[1,128,128]{2,1,0:T(8,128)S(1)} %fusion.54), custom_call_target="InvertDiagBlocksLowerTriangular" | custom-call | tf_op jit(solution)/shard_map/triangular_solve/custom-call.0 | solution.py:32
  686.1 11.7 %custom-call.30 = f32[128,128]{1,0:T(8,128)S(1)} custom-call(f32[128,128]{1,0:T(8,128)S(1)} %slice.145), custom_call_target="Cholesky" | custom-call | tf_op jit(solution)/shard_map/cholesky/custom-call.1 | solution.py:31
  699.1 10.0 %custom-call.31 = f32[1,128,128]{1,2,0:T(8,128)S(1)} custom-call(f32[1,128,128]{2,1,0:T(8,128)S(1)} %fusion.55), custom_call_target="InvertDiagBlocksLowerTriangular" | custom-call | tf_op jit(solution)/shard_map/triangular_solve/custom-call.0 | solution.py:32
  710.7 11.7 %custom-call.32 = f32[128,128]{1,0:T(8,128)S(1)} custom-call(f32[128,128]{1,0:T(8,128)S(1)} %slice.150), custom_call_target="Cholesky" | custom-call | tf_op jit(solution)/shard_map/cholesky/custom-call.1 | solution.py:31
  723.7 9.8 %custom-call.33 = f32[1,128,128]{1,2,0:T(8,128)S(1)} custom-call(f32[1,128,128]{2,1,0:T(8,128)S(1)} %fusion.56), custom_call_target="InvertDiagBlocksLowerTriangular" | custom-call | tf_op jit(solution)/shard_map/triangular_solve/custom-call.0 | solution.py:32
  734.4 11.7 %custom-call.34 = f32[128,128]{1,0:T(8,128)S(1)} custom-call(f32[128,128]{1,0:T(8,128)S(1)} %convolution_subtract_fusion.8), custom_call_target="Cholesky" | custom-call | tf_op jit(solution)/shard_map/cholesky/custom-call.1 | solution.py:31
  747.6 9.8 %custom-call.35 = f32[1,128,128]{1,2,0:T(8,128)S(1)} custom-call(f32[1,128,128]{2,1,0:T(8,128)S(1)} %fusion.57), custom_call_target="InvertDiagBlocksLowerTriangular" | custom-call | tf_op jit(solution)/shard_map/triangular_solve/custom-call.0 | solution.py:32
  765.0 10.9 %fusion.25 = f32[2048,512]{0,1:T(8,128)} fusion(f32[1024,128]{0,1:T(8,128)S(1)} %fusion.79, f32[1024,128]{0,1:T(8,128)S(1)} %fusion.13, f32[1024,128]{0,1:T(8,128)S(1)} %fusion.15, f32[1024,128]{0,1:T(8,128)S(1)} %fusion.17, f32[1024,2048]{1,0:T(8,128)} %param.7, bf16[1024,2048]{1,0:T(8,128)(2,1)S(1)} %copy-done.1), kind=kOutput, calls=%fused_computation.43 | convolution fusion | flops 6448218112 | bytes 18874368 | tf_op jit(solution)/shard_map/dot_general | solution.py:56
  776.0 88.0 %reduce-scatter.5.cloned.1.call-done = f32[2048,64]{0,1:T(8,128)} async-done(((f32[2048,512]{0,1:T(8,128)}), f32[2048,64]{0,1:T(8,128)}) %reduce-scatter.5.cloned.1.call-update) | async-done | bytes 524304 | tf_op jit(solution)/shard_map/reduce_scatter | solution.py:59
  871.5 21.6 %all-reduce.1 = f32[512]{0:T(512)S(1)} all-reduce(f32[512]{0:T(512)S(1)} %fusion.74), channel_id=1, replica_groups=mesh['row'=8,'col'=4] {'row'}, use_global_device_ids=true, to_apply=%add.1 | all-reduce | flops 512 | bytes 4096
  895.0 43.9 %all-gather.8.cloned.1.call-done = f32[2048,512]{0,1:T(8,128)} async-done(((f32[2048,64]{0,1:T(8,128)}), f32[2048,512]{0,1:T(8,128)}) %all-gather.8.cloned.1.call-update) | async-done | bytes 4194320 | tf_op jit(solution)/shard_map/all_gather | solution.py:64
  938.9 13.9 %multiply_subtract_fusion = f32[1024,2048]{1,0:T(8,128)} fusion(f32[2048,512]{0,1:T(8,128)} %all-gather.8.cloned.1.call-done, f32[1024,128]{0,1:T(8,128)S(1)} %fusion.79, f32[1024,128]{0,1:T(8,128)S(1)} %fusion.13, f32[1024,128]{0,1:T(8,128)S(1)} %fusion.15, f32[1024,128]{0,1:T(8,128)S(1)} %fusion.17, f32[1024,2048]{1,0:T(8,128)} %param.7, ...), kind=kOutput, calls=%fused_computation.1 | convolution fusion | flops 6452412416 | bytes 27262976 | tf_op jit(solution)/shard_map/dot_general | solution.py:69
  (116 shorter events, 79.1 us)
Async XLA Ops:
  7.2 78.5 %all-gather.4.cloned.1.call-start = ((), (), s32[]{:S(2)}) async-start(), calls=%async_computation.2 | async-start | bytes 4718592 | tf_op jit(solution)/shard_map/all_gather | solution.py:49
  7.9 139.8 %all-reduce.7.cloned.1.call-start = ((), (), s32[]{:S(2)}) async-start(), calls=%async_computation.3 | async-start | bytes 4194304 | tf_op jit(solution)/shard_map/psum | solution.py:53
  97.7 135.3 %all-reduce.9.cloned.1.call-start = ((), (), s32[]{:S(2)}) async-start(), calls=%async_computation.4 | async-start | bytes 2097152 | tf_op jit(solution)/shard_map/psum | solution.py:54
  154.4 176.8 %copy-start.2 = (f32[1024,512]{1,0:T(8,128)S(1)}, f32[1024,512]{1,0:T(8,128)}, u32[]{:S(2)}) copy-start(f32[1024,512]{1,0:T(8,128)} %all-reduce.7.cloned.1.call-done) | copy-start | bytes 6291460
  154.4 282.4 %reduce-scatter.3.cloned.1.call-start = ((), (), s32[]{:S(2)}) async-start(), calls=%async_computation.5 | async-start | bytes 4718592 | tf_op jit(solution)/shard_map/reduce_scatter | solution.py:59
  333.7 3.9 copy-start
  348.7 88.2 %copy-start.9 = (u32[32]{0:T(128)S(1)}, u32[32]{0:T(128)}, u32[]{:S(2)}) copy-start(u32[32]{0:T(128)} %constant.27) | copy-start | bytes 388
  348.8 162.8 %all-gather.6.cloned.1.call-start = ((), (), s32[]{:S(2)}) async-start(), calls=%async_computation.6 | async-start | bytes 4718592 | tf_op jit(solution)/shard_map/all_gather | solution.py:64
  436.8 137.0 %all-reduce.11.cloned.1.call-start = ((), (), s32[]{:S(2)}) async-start(), calls=%async_computation.7 | async-start | bytes 4194304 | tf_op jit(solution)/shard_map/psum | solution.py:53
  523.8 135.3 %all-reduce.13.cloned.1.call-start = ((), (), s32[]{:S(2)}) async-start(), calls=%async_computation.8 | async-start | bytes 2097152 | tf_op jit(solution)/shard_map/psum | solution.py:54
  580.5 177.2 %copy-start.3 = (f32[1024,512]{1,0:T(8,128)S(1)}, f32[1024,512]{1,0:T(8,128)}, u32[]{:S(2)}) copy-start(f32[1024,512]{1,0:T(8,128)} %all-reduce.11.cloned.1.call-done) | copy-start | bytes 6291460
  580.5 283.5 %reduce-scatter.5.cloned.1.call-start = ((), (), s32[]{:S(2)}) async-start(), calls=%async_computation.9 | async-start | bytes 4718592 | tf_op jit(solution)/shard_map/reduce_scatter | solution.py:59
  683.0 26.3 %copy-start.5 = (f32[128,128]{1,0:T(8,128)}, f32[128,128]{1,0:T(8,128)S(1)}, u32[]{:S(2)}) copy-start(f32[128,128]{1,0:T(8,128)S(1)} %fusion.32) | copy-start | bytes 196612
  709.4 0.6 copy-start.6
  710.7 50.4 %copy-start.7 = (f32[128,128]{1,0:T(8,128)S(1)}, f32[128,128]{1,0:T(8,128)}, u32[]{:S(2)}) copy-start(f32[128,128]{1,0:T(8,128)} %copy-done.6) | copy-start | bytes 196612
  761.1 3.9 copy-start.1
  775.9 162.9 %all-gather.8.cloned.1.call-start = ((), (), s32[]{:S(2)}) async-start(), calls=%async_computation.10 | async-start | bytes 4718592 | tf_op jit(solution)/shard_map/all_gather | solution.py:64
  938.9 13.9 %copy-start.4 = (f32[2048,512]{0,1:T(8,128)S(1)}, f32[2048,512]{0,1:T(8,128)}, u32[]{:S(2)}) copy-start(f32[2048,512]{0,1:T(8,128)} %all-gather.8.cloned.1.call-done) | copy-start | bytes 12582916
  938.9 13.9 %copy-start.8 = (bf16[1024,2048]{1,0:T(8,128)(2,1)S(1)}, bf16[1024,2048]{1,0:T(8,128)(2,1)}, u32[]{:S(2)}) copy-start(bf16[1024,2048]{1,0:T(8,128)(2,1)} %param.9) | copy-start | bytes 12582916
Sparse Core Ops, SparseCore 0:
  10.1 75.5 all-gather.3
  97.8 49.9 all-reduce.6
  154.5 78.3 all-reduce.8
  348.9 87.8 reduce-scatter.2
  438.8 72.7 all-gather.5
  523.9 49.8 all-reduce.10
  580.6 78.3 all-reduce.12
  776.0 87.8 reduce-scatter.4
  866.1 72.6 all-gather.7
where the time goes:
time: 975 us; the launch traced here: 969 us
  waiting for transfers between devices  599 us (61%)
  other arithmetic  188 us (19%)
  matrix products  107 us (11%)
  blocking collectives  55.5 us (6%)
  between operations  15.6 us (2%)
    reduce_scatter x2, waiting for transfers between devices, shards(): lax.psum_scatter(transposed, 'row', scatter_dimension=1, tiled=True)  176 us
    psum x2, waiting for transfers between devices, shards(): gram_sum = lax.psum(self_gram(left_sum), 'row')  156 us
    psum x2, waiting for transfers between devices, shards(): left_sum = lax.psum(partials, 'col')  100 us
    another operation x24, other arithmetic, solve_rows(): corner = lax.linalg.cholesky(trailing[:size, :size], symmetrize_input=False)  99.1 us
    all_gather x2, waiting for transfers between devices, shards(): lax.all_gather(products, 'row', axis=1, tiled=True)  88.2 us
    another operation x16, other arithmetic, solve_rows(): lax.linalg.triangular_solve(corner, jnp.eye(size, dtype=corner.dtype), le...  84.4 us
    all_gather x1, waiting for transfers between devices, shards(): right_full = lax.all_gather(right_start, 'row', axis=1, tiled=True)  77.7 us
    unnamed x2, blocking collectives  43.1 us
  transfers between devices with their start and end apart: 9, of which 9 were waited for; matrix products, arithmetic and copies ran while one was open for 1% of the time, Pallas kernels for 0%

commit v1 on v0

--- a/solution.py
+++ b/solution.py
@@ -10,6 +10,22 @@
 momentum_decay = 0.9
 step_rate = 0.1
 epsilon = 1e-06
+
+
+def _resolve_patches(inp, chip_axis):
+    n_parts = lax.axis_size(chip_axis)
+
+    def trace_shards(current_value, y1):
+        if y1 >= n_parts:
+            return current_value
+        pile = []
+        for s in range(n_parts):
+            pile.append((s, s ^ y1))
+        return trace_shards(
+            current_value + lax.ppermute(current_value, axis_name=chip_axis, perm=pile), 2 * y1
+        )
+
+    return trace_shards(inp, 1)
 
 
 def self_gram(rows):
@@ -50,7 +66,7 @@
     right_shard = right_start
     for iteration in range(ITERS):
         partials = jnp.dot(blended, right_full, precision=wide_mode)
-        left_sum = lax.psum(partials, "col")
+        left_sum = _resolve_patches(partials, "col")
         gram_sum = lax.psum(self_gram(left_sum), "row")
         left_rows = solve_rows(left_sum, gram_sum)
         transposed = lax.dot_general(

time: 975 us -> 976 us (level)
    ppermute x0 -> x4, waiting for transfers between devices: none -> 101 us  [trace_shards(): lax.ppermute(current_value, axis_name=chip_axis, perm=pile)]
    psum x2 -> x0, waiting for transfers between devices: 100 us -> none  [shards(): left_sum = lax.psum(partials, 'col')]
  transfers between devices with their start and end apart: 9 -> 11, of which waited for: 9 -> 11; matrix products, arithmetic and copies ran while one was open for 1% -> 1% of each run, Pallas kernels for 0% -> 0%
where the time goes in v1:
time: 976 us; the launch traced here: 968 us
  waiting for transfers between devices  597 us (61%)
  other arithmetic  190 us (19%)
  matrix products  101 us (10%)
  blocking collectives  55.5 us (6%)
  between operations  15.8 us (2%)
    reduce_scatter x2, waiting for transfers between devices, shards(): lax.psum_scatter(transposed, 'row', scatter_dimension=1, tiled=True)  176 us
    psum x2, waiting for transfers between devices, shards(): gram_sum = lax.psum(self_gram(left_sum), 'row')  153 us
    ppermute x4, waiting for transfers between devices, trace_shards(): lax.ppermute(current_value, axis_name=chip_axis, perm=pile)  101 us
    another operation x24, other arithmetic, solve_rows(): corner = lax.linalg.cholesky(trailing[:size, :size], symmetrize_input=False)  99.5 us
    all_gather x2, waiting for transfers between devices, shards(): lax.all_gather(products, 'row', axis=1, tiled=True)  88.2 us
    another operation x16, other arithmetic, solve_rows(): lax.linalg.triangular_solve(corner, jnp.eye(size, dtype=corner.dtype), le...  84.3 us
    all_gather x1, waiting for transfers between devices, shards(): right_full = lax.all_gather(right_start, 'row', axis=1, tiled=True)  77.7 us
    unnamed x2, blocking collectives  43.2 us
  transfers between devices with their start and end apart: 11, of which 11 were waited for; matrix products, arithmetic and copies ran while one was open for 1% of the time, Pallas kernels for 0%

profile of v1, /device:TPU:0, one launch (start us, length us, event | category | flops | bytes accessed | tf_op | source)
XLA Modules:
  0.0 968.5 jit_solution(9608625235965745001)
XLA Ops:
  7.9 77.7 %all-gather.4.cloned.1.call-done = f32[2048,512]{0,1:T(8,128)} async-done(((f32[2048,64]{0,1:T(8,128)}), f32[2048,512]{0,1:T(8,128)}) %all-gather.4.cloned.1.call-update) | async-done | bytes 4194320 | tf_op jit(solution)/shard_map/all_gather | solution.py:65
  85.7 11.0 %fusion.77 = f32[1024,512]{1,0:T(8,128)S(1)} fusion(f32[2048,512]{0,1:T(8,128)} %all-gather.4.cloned.1.call-done, f32[1024,2048]{1,0:T(8,128)} %param.7, bf16[1024,2048]{1,0:T(8,128)(2,1)} %param.8), kind=kOutput, calls=%fused_computation.124 | convolution fusion | flops 6446645248 | bytes 18874368 | tf_op jit(solution)/shard_map/dot_general | solution.py:68
  102.9 46.2 %collective-permute-done.1 = f32[1024,512]{1,0:T(8,128)S(1)} collective-permute-done((f32[1024,512]{1,0:T(8,128)S(1)}, f32[1024,512]{1,0:T(8,128)S(1)}, u32[]{:S(2)}, u32[]{:S(2)}) %collective-permute-start.1) | collective-permute-done | bytes 2097184 | tf_op jit(solution)/shard_map/ppermute | solution.py:25
  154.4 76.8 %all-reduce.5.cloned.1.call-done = f32[512,512]{1,0:T(8,128)} async-done(((f32[512,512]{1,0:T(8,128)}), f32[512,512]{1,0:T(8,128)}) %all-reduce.5.cloned.1.call-update) | async-done | bytes 1048592 | tf_op jit(solution)/shard_map/psum | solution.py:70
  232.0 11.7 %custom-call.20 = f32[128,128]{1,0:T(8,128)S(1)} custom-call(f32[128,128]{1,0:T(8,128)S(1)} %slice.125), custom_call_target="Cholesky" | custom-call | tf_op jit(solution)/shard_map/cholesky/custom-call.1 | solution.py:47
  245.1 9.8 %custom-call.21 = f32[1,128,128]{1,2,0:T(8,128)S(1)} custom-call(f32[1,128,128]{2,1,0:T(8,128)S(1)} %fusion.52), custom_call_target="InvertDiagBlocksLowerTriangular" | custom-call | tf_op jit(solution)/shard_map/triangular_solve/custom-call.0 | solution.py:48
  257.8 11.7 %custom-call.22 = f32[128,128]{1,0:T(8,128)S(1)} custom-call(f32[128,128]{1,0:T(8,128)S(1)} %slice.130), custom_call_target="Cholesky" | custom-call | tf_op jit(solution)/shard_map/cholesky/custom-call.1 | solution.py:47
  270.8 10.2 %custom-call.23 = f32[1,128,128]{1,2,0:T(8,128)S(1)} custom-call(f32[1,128,128]{2,1,0:T(8,128)S(1)} %fusion.53), custom_call_target="InvertDiagBlocksLowerTriangular" | custom-call | tf_op jit(solution)/shard_map/triangular_solve/custom-call.0 | solution.py:48
  283.3 11.7 %custom-call.24 = f32[128,128]{1,0:T(8,128)S(1)} custom-call(f32[128,128]{1,0:T(8,128)S(1)} %slice.135), custom_call_target="Cholesky" | custom-call | tf_op jit(solution)/shard_map/cholesky/custom-call.1 | solution.py:47
  296.4 9.8 %custom-call.25 = f32[1,128,128]{1,2,0:T(8,128)S(1)} custom-call(f32[1,128,128]{2,1,0:T(8,128)S(1)} %fusion.54), custom_call_target="InvertDiagBlocksLowerTriangular" | custom-call | tf_op jit(solution)/shard_map/triangular_solve/custom-call.0 | solution.py:48
  308.7 11.9 %custom-call.26 = f32[128,128]{1,0:T(8,128)S(1)} custom-call(f32[128,128]{1,0:T(8,128)S(1)} %convolution_subtract_fusion.3), custom_call_target="Cholesky" | custom-call | tf_op jit(solution)/shard_map/cholesky/custom-call.1 | solution.py:47
  321.9 9.8 %custom-call.27 = f32[1,128,128]{1,2,0:T(8,128)S(1)} custom-call(f32[1,128,128]{2,1,0:T(8,128)S(1)} %fusion.55), custom_call_target="InvertDiagBlocksLowerTriangular" | custom-call | tf_op jit(solution)/shard_map/triangular_solve/custom-call.0 | solution.py:48
  337.9 11.0 %fusion.3 = f32[2048,512]{0,1:T(8,128)} fusion(f32[1024,128]{0,1:T(8,128)S(1)} %fusion.20, f32[1024,128]{0,1:T(8,128)S(1)} %fusion.21, f32[1024,128]{0,1:T(8,128)S(1)} %fusion.23, f32[1024,128]{0,1:T(8,128)S(1)} %fusion.25, f32[1024,2048]{1,0:T(8,128)} %param.7, bf16[1024,2048]{1,0:T(8,128)(2,1)S(1)} %copy-done), kind=kOutput, calls=%fused_computation.6 | convolution fusion | flops 6448218112 | bytes 18874368 | tf_op jit(solution)/shard_map/dot_general | solution.py:72
  349.0 88.0 %reduce-scatter.3.cloned.1.call-done = f32[2048,64]{0,1:T(8,128)} async-done(((f32[2048,512]{0,1:T(8,128)}), f32[2048,64]{0,1:T(8,128)}) %reduce-scatter.3.cloned.1.call-update) | async-done | bytes 524304 | tf_op jit(solution)/shard_map/reduce_scatter | solution.py:75
  445.8 21.6 %all-reduce = f32[512]{0:T(512)S(1)} all-reduce(f32[512]{0:T(512)S(1)} %bitcast_dynamic-update-slice_fusion), channel_id=1, replica_groups=mesh['row'=8,'col'=4] {'row'}, use_global_device_ids=true, to_apply=%add | all-reduce | flops 512 | bytes 4096
  467.3 44.4 %all-gather.6.cloned.1.call-done = f32[2048,512]{0,1:T(8,128)} async-done(((f32[2048,64]{0,1:T(8,128)}), f32[2048,512]{0,1:T(8,128)}) %all-gather.6.cloned.1.call-update) | async-done | bytes 4194320 | tf_op jit(solution)/shard_map/all_gather | solution.py:80
  511.7 11.2 %fusion.1 = f32[1024,512]{1,0:T(8,128)S(1)} fusion(f32[2048,512]{0,1:T(8,128)} %all-gather.6.cloned.1.call-done, f32[512]{0:T(512)S(1)} %all-reduce, f32[1024,2048]{1,0:T(8,128)} %param.7, bf16[1024,2048]{1,0:T(8,128)(2,1)} %param.8), kind=kOutput, calls=%fused_computation.4 | convolution fusion | flops 6447693824 | bytes 18876416 | tf_op jit(solution)/shard_map/dot_general | solution.py:68
  529.2 46.2 %collective-permute-done.3 = f32[1024,512]{1,0:T(8,128)S(1)} collective-permute-done((f32[1024,512]{1,0:T(8,128)S(1)}, f32[1024,512]{1,0:T(8,128)S(1)}, u32[]{:S(2)}, u32[]{:S(2)}) %collective-permute-start.3) | collective-permute-done | bytes 2097184 | tf_op jit(solution)/shard_map/ppermute | solution.py:25
  580.9 76.6 %all-reduce.7.cloned.1.call-done = f32[512,512]{1,0:T(8,128)} async-done(((f32[512,512]{1,0:T(8,128)}), f32[512,512]{1,0:T(8,128)}) %all-reduce.7.cloned.1.call-update) | async-done | bytes 1048592 | tf_op jit(solution)/shard_map/psum | solution.py:70
  658.3 11.7 %custom-call.28 = f32[128,128]{1,0:T(8,128)S(1)} custom-call(f32[128,128]{1,0:T(8,128)S(1)} %slice.140), custom_call_target="Cholesky" | custom-call | tf_op jit(solution)/shard_map/cholesky/custom-call.1 | solution.py:47
  671.4 9.8 %custom-call.29 = f32[1,128,128]{1,2,0:T(8,128)S(1)} custom-call(f32[1,128,128]{2,1,0:T(8,128)S(1)} %fusion.56), custom_call_target="InvertDiagBlocksLowerTriangular" | custom-call | tf_op jit(solution)/shard_map/triangular_solve/custom-call.0 | solution.py:48
  684.0 11.7 %custom-call.30 = f32[128,128]{1,0:T(8,128)S(1)} custom-call(f32[128,128]{1,0:T(8,128)S(1)} %slice.145), custom_call_target="Cholesky" | custom-call | tf_op jit(solution)/shard_map/cholesky/custom-call.1 | solution.py:47
  697.1 10.0 %custom-call.31 = f32[1,128,128]{1,2,0:T(8,128)S(1)} custom-call(f32[1,128,128]{2,1,0:T(8,128)S(1)} %fusion.57), custom_call_target="InvertDiagBlocksLowerTriangular" | custom-call | tf_op jit(solution)/shard_map/triangular_solve/custom-call.0 | solution.py:48
  709.3 11.7 %custom-call.32 = f32[128,128]{1,0:T(8,128)S(1)} custom-call(f32[128,128]{1,0:T(8,128)S(1)} %slice.150), custom_call_target="Cholesky" | custom-call | tf_op jit(solution)/shard_map/cholesky/custom-call.1 | solution.py:47
  722.5 9.8 %custom-call.33 = f32[1,128,128]{1,2,0:T(8,128)S(1)} custom-call(f32[1,128,128]{2,1,0:T(8,128)S(1)} %fusion.58), custom_call_target="InvertDiagBlocksLowerTriangular" | custom-call | tf_op jit(solution)/shard_map/triangular_solve/custom-call.0 | solution.py:48
  734.9 11.9 %custom-call.34 = f32[128,128]{1,0:T(8,128)S(1)} custom-call(f32[128,128]{1,0:T(8,128)S(1)} %convolution_subtract_fusion.2), custom_call_target="Cholesky" | custom-call | tf_op jit(solution)/shard_map/cholesky/custom-call.1 | solution.py:47
  748.1 9.8 %custom-call.35 = f32[1,128,128]{1,2,0:T(8,128)S(1)} custom-call(f32[1,128,128]{2,1,0:T(8,128)S(1)} %fusion.59), custom_call_target="InvertDiagBlocksLowerTriangular" | custom-call | tf_op jit(solution)/shard_map/triangular_solve/custom-call.0 | solution.py:48
  764.1 10.9 %fusion.27 = f32[2048,512]{0,1:T(8,128)} fusion(f32[1024,128]{0,1:T(8,128)S(1)} %fusion.13, f32[1024,128]{0,1:T(8,128)S(1)} %fusion.14, f32[1024,128]{0,1:T(8,128)S(1)} %fusion.16, f32[1024,128]{0,1:T(8,128)S(1)} %fusion.18, f32[1024,2048]{1,0:T(8,128)} %param.7, bf16[1024,2048]{1,0:T(8,128)(2,1)S(1)} %copy-done.1), kind=kOutput, calls=%fused_computation.45 | convolution fusion | flops 6448218112 | bytes 18874368 | tf_op jit(solution)/shard_map/dot_general | solution.py:72
  775.0 88.0 %reduce-scatter.5.cloned.1.call-done = f32[2048,64]{0,1:T(8,128)} async-done(((f32[2048,512]{0,1:T(8,128)}), f32[2048,64]{0,1:T(8,128)}) %reduce-scatter.5.cloned.1.call-update) | async-done | bytes 524304 | tf_op jit(solution)/shard_map/reduce_scatter | solution.py:75
  870.5 21.6 %all-reduce.1 = f32[512]{0:T(512)S(1)} all-reduce(f32[512]{0:T(512)S(1)} %fusion.76), channel_id=1, replica_groups=mesh['row'=8,'col'=4] {'row'}, use_global_device_ids=true, to_apply=%add.1 | all-reduce | flops 512 | bytes 4096
  894.1 43.8 %all-gather.8.cloned.1.call-done = f32[2048,512]{0,1:T(8,128)} async-done(((f32[2048,64]{0,1:T(8,128)}), f32[2048,512]{0,1:T(8,128)}) %all-gather.8.cloned.1.call-update) | async-done | bytes 4194320 | tf_op jit(solution)/shard_map/all_gather | solution.py:80
  937.9 13.9 %multiply_subtract_fusion = f32[1024,2048]{1,0:T(8,128)} fusion(f32[2048,512]{0,1:T(8,128)} %all-gather.8.cloned.1.call-done, f32[1024,128]{0,1:T(8,128)S(1)} %fusion.13, f32[1024,128]{0,1:T(8,128)S(1)} %fusion.14, f32[1024,128]{0,1:T(8,128)S(1)} %fusion.16, f32[1024,128]{0,1:T(8,128)S(1)} %fusion.18, f32[1024,2048]{1,0:T(8,128)} %param.7, ...), kind=kOutput, calls=%fused_computation.1 | convolution fusion | flops 6452412416 | bytes 27262976 | tf_op jit(solution)/shard_map/dot_general | solution.py:85
  (128 shorter events, 90.7 us)
Async XLA Ops:
  7.2 78.5 %all-gather.4.cloned.1.call-start = ((), (), s32[]{:S(2)}) async-start(), calls=%async_computation.2 | async-start | bytes 4718592 | tf_op jit(solution)/shard_map/all_gather | solution.py:65
  7.9 223.3 %all-reduce.5.cloned.1.call-start = ((), (), s32[]{:S(2)}) async-start(), calls=%async_computation.3 | async-start | bytes 2097152 | tf_op jit(solution)/shard_map/psum | solution.py:70
  96.7 4.2 collective-permute-start
  101.4 47.7 %collective-permute-start.1 = (f32[1024,512]{1,0:T(8,128)S(1)}, f32[1024,512]{1,0:T(8,128)S(1)}, u32[]{:S(2)}, u32[]{:S(2)}) collective-permute-start(f32[1024,512]{1,0:T(8,128)S(1)} %add.38), channel_id=1, source_target_pairs={{0,2},{1,3},{2,0},{3,1},{4,6},{5,7},{6,4},{7,5},{8,10},{9,11},{10,... | collective-permute-start | bytes 6291464 | tf_op jit(solution)/shard_map/ppermute | solution.py:25
  154.1 282.9 %reduce-scatter.3.cloned.1.call-start = ((), (), s32[]{:S(2)}) async-start(), calls=%async_computation.4 | async-start | bytes 4718592 | tf_op jit(solution)/shard_map/reduce_scatter | solution.py:75
  254.9 2.2 copy-start.5
  281.3 0.6 copy-start.7
  282.6 0.7 copy-start.3
  320.6 13.4 %copy-start.8 = (f32[128,128]{1,0:T(8,128)S(1)}, f32[128,128]{1,0:T(8,128)}, u32[]{:S(2)}) copy-start(f32[128,128]{1,0:T(8,128)} %copy-done.7) | copy-start | bytes 196612
  334.5 3.3 copy-start
  348.9 88.2 %copy-start.12 = (u32[32]{0:T(128)S(1)}, u32[32]{0:T(128)}, u32[]{:S(2)}) copy-start(u32[32]{0:T(128)} %constant.27) | copy-start | bytes 388
  348.9 162.8 %all-gather.6.cloned.1.call-start = ((), (), s32[]{:S(2)}) async-start(), calls=%async_computation.5 | async-start | bytes 4718592 | tf_op jit(solution)/shard_map/all_gather | solution.py:80
  437.0 220.5 %all-reduce.7.cloned.1.call-start = ((), (), s32[]{:S(2)}) async-start(), calls=%async_computation.6 | async-start | bytes 2097152 | tf_op jit(solution)/shard_map/psum | solution.py:70
  523.0 4.2 collective-permute-start.2
  527.7 47.7 %collective-permute-start.3 = (f32[1024,512]{1,0:T(8,128)S(1)}, f32[1024,512]{1,0:T(8,128)S(1)}, u32[]{:S(2)}, u32[]{:S(2)}) collective-permute-start(f32[1024,512]{1,0:T(8,128)S(1)} %add.41), channel_id=1, source_target_pairs={{0,2},{1,3},{2,0},{3,1},{4,6},{5,7},{6,4},{7,5},{8,10},{9,11},{10,... | collective-permute-start | bytes 6291464 | tf_op jit(solution)/shard_map/ppermute | solution.py:25
  580.4 282.7 %reduce-scatter.5.cloned.1.call-start = ((), (), s32[]{:S(2)}) async-start(), calls=%async_computation.7 | async-start | bytes 4718592 | tf_op jit(solution)/shard_map/reduce_scatter | solution.py:75
  681.2 2.2 copy-start.6
  707.3 0.6 copy-start.9
  708.6 0.7 copy-start.4
  746.8 13.4 %copy-start.10 = (f32[128,128]{1,0:T(8,128)S(1)}, f32[128,128]{1,0:T(8,128)}, u32[]{:S(2)}) copy-start(f32[128,128]{1,0:T(8,128)} %copy-done.9) | copy-start | bytes 196612
  760.7 3.3 copy-start.1
  775.0 162.9 %all-gather.8.cloned.1.call-start = ((), (), s32[]{:S(2)}) async-start(), calls=%async_computation.8 | async-start | bytes 4718592 | tf_op jit(solution)/shard_map/all_gather | solution.py:80
  937.9 14.0 %copy-start.2 = (f32[2048,512]{0,1:T(8,128)S(1)}, f32[2048,512]{0,1:T(8,128)}, u32[]{:S(2)}) copy-start(f32[2048,512]{0,1:T(8,128)} %all-gather.8.cloned.1.call-done) | copy-start | bytes 12582916
  937.9 14.0 %copy-start.11 = (bf16[1024,2048]{1,0:T(8,128)(2,1)S(1)}, bf16[1024,2048]{1,0:T(8,128)(2,1)}, u32[]{:S(2)}) copy-start(bf16[1024,2048]{1,0:T(8,128)(2,1)} %param.9) | copy-start | bytes 12582916
Sparse Core Ops, SparseCore 0:
  10.1 75.5 all-gather.3
  154.2 76.8 all-reduce.4
  349.0 87.8 reduce-scatter.2
  439.0 72.7 all-gather.5
  580.5 76.8 all-reduce.6
  775.1 87.8 reduce-scatter.4
  865.2 72.6 all-gather.7
